TPU v7x, 32 devices: a whole 2x2x4 slice. The times are simulated.
32 devices in a mesh: dom: 32 (over z, y, x, core).
Axes of the slice: x: 2, y: 2, z: 4, core: 2. Of those that a mesh axis runs over, the one named last changes fastest.
Arguments:
- rest_pos: float32 [3, 131072], P(None, 'dom'), may hold values from -6 to 6
- displacement: float32 [3, 131072], P(None, 'dom'), may hold values from -3 to 3
- velocity: float32 [3, 131072], P(None, 'dom'), may hold values from -6 to 6
- ext_force: float32 [3, 131072], P(None, 'dom'), may hold values from -6 to 6
- node_mass: float32 [131072], P('dom'), may hold values from 0.5 to 2
- body_accel: float32 [3], replicated, may hold values from -2 to 2
- connectivity: int32 [8, 131072], P(None, 'dom'), may hold values from 0 to 4095
- elem_material: int32 [1024], P('dom'), may hold values from 0 to 7
- stiffness: float32 [8, 24, 24], replicated, may hold values from -1.25 to 1.25
- shared_nodes: int32 [32, 5, 128], P('dom'), may hold values from 0 to 4095, as said below
- contact_slave: int32 [65536], P('dom'), may hold values from 0 to 4095
- contact_owner: int32 [65536, 1], P('dom'), may hold values from 0 to 31; in each aligned block of 2048 rows (0 to 2047, 2048 to 4095, ...) at most 256 rows name the same one
- contact_master: int32 [65536], P('dom'), may hold values from 0 to 4095
- contact_normal: float32 [3, 65536], P(None, 'dom'), may hold values from -4 to 4
- part_of_node: int32 [131072], P('dom'), may hold values from 0 to 799
- part_mass: float32 [400], replicated, may hold values from 81 to 327
- part_center: float32 [3, 400], replicated, may hold values from -1 to 1
- part_inertia: float32 [3, 400], replicated, may hold values from 81 to 327
Outputs:
- nodal_velocity: float32 [3, 131072], P(None, 'dom')
- part_motion: float32 [6, 400], replicated
Inputs may be any that keep to these rules, and one draw needn't show every extreme that they name: `connectivity`: offsets are taken modulo 4096 after adding the element's own local number. `shared_nodes`: on each partition d the 5 x 128 entries are distinct interface copies; entry k of list b on d and entry k of list b on d XOR 2**b are copies of one node. `contact_slave`: slave indices are local copies of the contact's own partition. `contact_owner`: among the 2048 contacts of one partition no owner appears more than 256 times, and some owner appears exactly 256 times. `contact_master`: master indices are local copies of the owner partition. `part_of_node`: values of 400 or more mark copies of no rigid part.
All inputs are finite; a program needn't handle non-finite values.
Results may differ from a plain program's by a relative error of at most 0.0001.
Values sent between devices are 32-bit elements; how exact they have to be, the bound alone decides.
A program may use at most 128 MiB of HBM per device.

v0:
```python
import jax
import jax.numpy as jnp
from jax import lax
from jax.sharding import PartitionSpec as P

CYCLES = 3
PARTS_SIZE = 400
TIME_STEP = 0.1
DAMP_RATIO = 0.05
PENALTY = 2.0
GAP_WIDTH = 0.5
CONTACT_DAMP = 0.2


def partner(block, axis, apart):
    count = lax.axis_size(axis)
    route = []
    for low in range(count):
        high = low | 1 << apart
        if high != low and high < count:
            route += [(low, high), (high, low)]
    return lax.ppermute(block, axis, route)


def element_forces(corners, material, stiffness, nodal_field):
    blocks = corners.shape[1] // 128
    material_count = stiffness.shape[0]
    onehot = (material[:, None] == jnp.arange(material_count, dtype=jnp.int32)[None, :]).astype(
        jnp.float32
    )
    block_matrix = jnp.dot(
        onehot, stiffness.reshape(material_count, 576), precision=lax.Precision.HIGHEST
    ).reshape(blocks, 24, 24)
    gathered = nodal_field[:, corners].reshape(24, blocks, 128)
    forces = jnp.einsum("bij,jbk->ibk", block_matrix, gathered, precision=lax.Precision.HIGHEST)
    return (
        jnp.zeros_like(nodal_field)
        .at[:, corners.reshape(-1)]
        .add(forces.reshape(3, 8 * corners.shape[1]))
    )


def contact_push(slave_pos, slave_vel, master_pos, master_vel, normal):
    gap_size = jnp.sum((slave_pos - master_pos) * normal, axis=0)
    closing = jnp.sum((slave_vel - master_vel) * normal, axis=0)
    push_size = (
        PENALTY * GAP_WIDTH * jax.nn.softplus(-gap_size / GAP_WIDTH) - CONTACT_DAMP * closing
    )
    return push_size[None] * normal


def cross_product(left, right):
    return jnp.stack(
        [
            left[1] * right[2] - left[2] * right[1],
            left[2] * right[0] - left[0] * right[2],
            left[0] * right[1] - left[1] * right[0],
        ]
    )


def per_device(
    rest_pos,
    displacement,
    velocity,
    ext_force,
    node_mass,
    body_accel,
    connectivity,
    elem_material,
    stiffness,
    shared_nodes,
    contact_slave,
    contact_owner,
    contact_master,
    contact_normal,
    part_of_node,
    part_mass,
    part_center,
    part_inertia,
):
    domains = lax.axis_size("dom")
    neighbours = shared_nodes.shape[1]
    shared_count = shared_nodes.shape[2]
    shared_flat = shared_nodes.reshape(-1)
    accel_column = body_accel[:, None]
    node_count = displacement.shape[1]
    local_elem = jnp.arange(connectivity.shape[1], dtype=jnp.int32)
    corners = (connectivity + local_elem[None, :]) % node_count
    displaced = displacement
    speeds = velocity
    assembled = jnp.zeros_like(displacement)
    for cycle_index in range(CYCLES):
        internal = element_forces(
            corners, elem_material, stiffness, displaced + DAMP_RATIO * speeds
        )
        own_values = internal[:, shared_flat].reshape(3, neighbours, shared_count)
        received = []
        for bit_number in range(neighbours):
            received.append(partner(own_values[:, bit_number], "dom", bit_number))
        assembled = internal.at[:, shared_flat].add(
            jnp.stack(received, axis=1).reshape(3, neighbours * shared_count)
        )
        speeds = speeds + TIME_STEP * ((ext_force - assembled) / node_mass[None] - accel_column)
        displaced = displaced + TIME_STEP * speeds
    positions = rest_pos + displaced
    contacts = contact_slave.shape[0]
    capacity = 4 * contacts // domains
    owners = contact_owner[:, 0]
    owner_hits = (owners[:, None] == jnp.arange(domains, dtype=jnp.int32)[None, :]).astype(
        jnp.int32
    )
    slot_rank = jnp.sum(jnp.cumsum(owner_hits, axis=0) * owner_hits, axis=1) - 1
    slot_index = owners * capacity + slot_rank
    slave_pos = positions[:, contact_slave]
    slave_vel = speeds[:, contact_slave]
    contact_force = jnp.zeros_like(positions)
    payload = jnp.zeros((10, domains * capacity), jnp.float32).at[9].set(-1.0)
    payload = payload.at[:, slot_index].set(
        jnp.concatenate(
            [slave_pos, slave_vel, contact_normal, contact_master[None].astype(jnp.float32)], 0
        )
    )
    payload = payload.reshape(10, domains, capacity)
    arrived = lax.all_to_all(payload, "dom", split_axis=1, concat_axis=1, tiled=True)
    valid_slot = (arrived[9] >= 0.0).astype(jnp.float32)
    master_index = jnp.maximum(arrived[9], 0.0).astype(jnp.int32)
    pushed = (
        contact_push(
            arrived[0:3],
            arrived[3:6],
            positions[:, master_index],
            speeds[:, master_index],
            arrived[6:9],
        )
        * valid_slot[None]
    )
    returned = lax.all_to_all(pushed, "dom", split_axis=1, concat_axis=1, tiled=True)
    returned, pushed, master_float = (returned, pushed, arrived[9:10])
    master_index = jnp.maximum(master_float, 0.0).astype(jnp.int32)
    contact_force = contact_force.at[:, master_index.reshape(-1)].add(-pushed.reshape(3, -1))
    slave_push = returned.reshape(3, domains * capacity)[:, slot_index]
    contact_force = contact_force.at[:, contact_slave].add(slave_push)
    nodal_velocity = speeds + TIME_STEP * contact_force / node_mass[None]
    net_force = ext_force - assembled + contact_force - node_mass[None] * accel_column
    part_index = jnp.minimum(part_of_node, PARTS_SIZE)
    weighted = jnp.concatenate([node_mass[None], node_mass[None] * positions], 0)
    totals = lax.psum(
        jax.ops.segment_sum(
            jnp.concatenate([weighted, net_force, cross_product(positions, net_force)], 0).T,
            part_index,
            PARTS_SIZE + 1,
        )[:PARTS_SIZE].T,
        "dom",
    )
    mass_total = part_mass + totals[0]
    centre = (part_mass[None] * part_center + totals[1:4]) / mass_total[None]
    force_sum = totals[4:7]
    torque = totals[7:10] - cross_product(centre, force_sum)
    part_motion = jnp.concatenate([force_sum / mass_total[None], torque / part_inertia], 0)
    return (nodal_velocity, part_motion)


def solution(mesh):
    placed = (
        P(None, "dom"),
        P(None, "dom"),
        P(None, "dom"),
        P(None, "dom"),
        P("dom"),
        P(),
        P(None, "dom"),
        P("dom"),
        P(),
        P("dom", None, None),
        P("dom"),
        P("dom", None),
        P("dom"),
        P(None, "dom"),
        P("dom"),
        P(),
        P(),
        P(),
    )
    return jax.shard_map(
        per_device, mesh=mesh, in_specs=placed, out_specs=(P(None, "dom"), P()), check_vma=False
    )
```

profile of v0, /device:TPU:0, one launch (start us, length us, event | category | flops | bytes accessed | tf_op | source)
XLA Modules:
  0.0 1264.1 jit_solution(16717740665865341079)
XLA Ops:
  5.1 109.0 %gather_fusion = f32[32768,3]{1,0:T(8,128)} fusion(f32[3,4096]{0,1:T(8,128)S(1)} %copy.282, s32[32768]{0:T(1024)S(1)} %broadcast_clamp_fusion), kind=kCustom, calls=%fused_computation | custom fusion | bytes 917504 | tf_op jit(solution)/shard_map/gather | solution.py:34
  114.1 9.8 copy.283
  125.3 8.6 copy.288
  133.9 174.7 %scatter_custom_fusion = f32[3,4096]{0,1:T(8,128)S(1)} fusion(s32[32768]{0:T(1024)S(1)} %bitcast.187, f32[32768,3]{1,0:T(8,128)} %copy.288, f32[]{:T(128)} %constant.76.clone.1), kind=kCustom, calls=%fused_computation.32 | custom fusion | flops 98304 | bytes 49664 | tf_op jit(solution)/shard_map/scatter-add | solution.py:39
  320.1 9.1 reduce-window.6
  333.0 7.7 scatter_fusion
  342.8 109.0 %gather_fusion.2 = f32[32768,3]{1,0:T(8,128)} fusion(f32[3,4096]{0,1:T(8,128)S(1)} %copy.296, s32[32768]{0:T(1024)S(1)} %broadcast_clamp_fusion), kind=kCustom, calls=%fused_computation.2 | custom fusion | bytes 917504 | tf_op jit(solution)/shard_map/gather | solution.py:34
  451.8 9.8 copy.297
  462.9 8.6 copy.301
  471.5 174.7 %scatter_custom_fusion.2 = f32[3,4096]{0,1:T(8,128)S(1)} fusion(s32[32768]{0:T(1024)S(1)} %bitcast.188, f32[32768,3]{1,0:T(8,128)} %copy.301, f32[]{:T(128)} %constant.76.clone.1), kind=kCustom, calls=%fused_computation.30 | custom fusion | flops 98304 | bytes 49664 | tf_op jit(solution)/shard_map/scatter-add | solution.py:39
  657.4 7.4 scatter_fusion.1
  666.2 109.0 %gather_fusion.4 = f32[32768,3]{1,0:T(8,128)} fusion(f32[3,4096]{0,1:T(8,128)S(1)} %copy.309, s32[32768]{0:T(1024)S(1)} %broadcast_clamp_fusion), kind=kCustom, calls=%fused_computation.4 | custom fusion | bytes 917504 | tf_op jit(solution)/shard_map/gather | solution.py:34
  775.2 9.8 copy.310
  786.3 8.6 copy.314
  794.9 174.7 %scatter_custom_fusion.4 = f32[3,4096]{0,1:T(8,128)S(1)} fusion(s32[32768]{0:T(1024)S(1)} %bitcast.189, f32[32768,3]{1,0:T(8,128)} %copy.314, f32[]{:T(128)} %constant.76.clone.1), kind=kCustom, calls=%fused_computation.28 | custom fusion | flops 98304 | bytes 49664 | tf_op jit(solution)/shard_map/scatter-add | solution.py:39
  1004.7 7.0 gather_fusion.6
  1013.9 9.8 scatter_fusion.3
  1029.9 15.6 %all-to-all-done = f32[10,32,256]{2,0,1:T(8,128)S(1)} async-done(((f32[10,32,256]{2,0,1:T(8,128)}), f32[10,32,256]{2,0,1:T(8,128)S(1)}, u32[]{:S(2)}, u32[]{:S(2)}) %all-to-all-start) | async-done | bytes 327712 | tf_op jit(solution)/shard_map/all_to_all | solution.py:125
  1045.6 29.5 %gather_fusion.8 = f32[8192,3]{1,0:T(8,128)} fusion(f32[3,4096]{0,1:T(8,128)} %copy.324, s32[8192]{0:T(1024)S(1)} %broadcast_clamp_fusion.1), kind=kCustom, calls=%fused_computation.8 | custom fusion | bytes 229376 | tf_op jit(solution)/shard_map/gather | solution.py:132
  1075.1 27.9 %gather_fusion.9 = f32[8192,3]{1,0:T(8,128)} fusion(f32[3,4096]{0,1:T(8,128)S(1)} %copy.325, s32[8192]{0:T(1024)S(1)} %broadcast_clamp_fusion.1), kind=kCustom, calls=%fused_computation.9 | custom fusion | bytes 229376 | tf_op jit(solution)/shard_map/gather | solution.py:133
  1115.3 56.1 %scatter_custom_fusion.7 = f32[3,4096]{0,1:T(8,128)S(1)} fusion(s32[8192]{0:T(1024)S(1)} %bitcast.201, f32[8192,3]{1,0:T(8,128)} %copy.335, f32[]{:T(128)} %constant.76.clone.1), kind=kCustom, calls=%fused_computation.26 | custom fusion | flops 24576 | bytes 49664 | tf_op jit(solution)/shard_map/scatter-add | solution.py:141
  1174.1 24.1 %scatter_custom_fusion.8 = f32[3,4096]{0,1:T(8,128)S(1)} fusion(f32[3,4096]{0,1:T(8,128)S(1)} %scatter_custom_fusion.7, s32[2048]{0:T(1024)} %get-tuple-element.61, f32[3,8192]{0,1:T(8,128)} %bitcast.166, s32[2048]{0:T(1024)S(1)} %broadcast_clamp_fusion.2), kind=kCustom, calls=%fused_computation.24 | custom fusion | flops 6144 | bytes 49152 | tf_op jit(solution)/shard_map/scatter-add | solution.py:143
  1200.4 22.4 %scatter_custom_fusion.9 = f32[401,10]{1,0:T(8,128)S(1)} fusion(s32[4096]{0:T(1024)S(1)} %broadcast_minimum_fusion, f32[4096,10]{1,0:T(8,128)S(1)} %copy.339, f32[]{:T(128)} %constant.76.clone.1), kind=kCustom, calls=%fused_computation.60 | custom fusion | flops 40960 | bytes 16044 | tf_op jit(solution)/shard_map/scatter-add | solution.py:149
  1222.9 40.1 %psum.7 = f32[10,400]{1,0:T(8,128)S(1)} all-reduce(f32[10,400]{1,0:T(8,128)S(1)} %bitcast.192), channel_id=1, replica_groups=mesh['dom'=32] {'dom'}, use_global_device_ids=true, to_apply=%region_15.16 | all-reduce | flops 4000 | bytes 32000 | tf_op jit(solution)/shard_map/psum | solution.py:148
  (205 shorter events, 99.3 us)
Async XLA Ops:
  133.8 186.2 %copy-start.9 = (s32[2048,1]{0,1:T(1,128)S(1)}, s32[2048,1]{0,1:T(1,128)}, u32[]{:S(2)}) copy-start(s32[2048,1]{0,1:T(1,128)} %param.31) | copy-start | bytes 24580
  133.9 176.5 %copy-start.4 = (s32[640]{0:T(1024)}, s32[640]{0:T(1024)S(1)}, u32[]{:S(2)}) copy-start(s32[640]{0:T(1024)S(1)} %fusion.33) | copy-start | bytes 7684
  133.9 186.2 %copy-start.13 = (s32[1024]{0:T(1024)}, s32[1024]{0:T(1024)S(1)}, u32[]{:S(2)}) copy-start(s32[1024]{0:T(1024)S(1)} %pad_clamp_fusion) | copy-start | bytes 12292
  311.0 19.7 %collective-permute-start = (f32[3,128]{1,0:T(4,128)}, f32[3,128]{1,0:T(4,128)}, u32[]{:S(2)}, u32[]{:S(2)}) collective-permute-start(f32[3,128]{1,0:T(4,128)} %bitcast.10), channel_id=1, source_target_pairs={{0,1},{1,0},{2,3},{3,2},{4,5},{5,4},{6,7},{7,6},{8,9},{9,8},{10,11... | collective-permute-start | bytes 4616 | tf_op jit(solution)/shard_map/ppermute | solution.py:22
  311.6 19.8 %collective-permute-start.1 = (f32[3,128]{1,0:T(4,128)S(1)}, f32[3,128]{1,0:T(4,128)}, u32[]{:S(2)}, u32[]{:S(2)}) collective-permute-start(f32[3,128]{1,0:T(4,128)S(1)} %bitcast.210), channel_id=1, source_target_pairs={{0,2},{2,0},{1,3},{3,1},{4,6},{6,4},{5,7},{7,5},{8,10},{10,8},{9,1... | collective-permute-start | bytes 4616 | tf_op jit(solution)/shard_map/ppermute | solution.py:22
  314.1 17.9 %collective-permute-start.2 = (f32[3,128]{1,0:T(4,128)S(1)}, f32[3,128]{1,0:T(4,128)S(1)}, u32[]{:S(2)}, u32[]{:S(2)}) collective-permute-start(f32[3,128]{1,0:T(4,128)S(1)} %bitcast.209), channel_id=1, source_target_pairs={{0,4},{4,0},{1,5},{5,1},{2,6},{6,2},{3,7},{7,3},{8,12},{12,8},{9,1... | collective-permute-start | bytes 4616 | tf_op jit(solution)/shard_map/ppermute | solution.py:22
  315.8 16.3 %collective-permute-start.3 = (f32[3,128]{1,0:T(4,128)S(1)}, f32[3,128]{1,0:T(4,128)S(1)}, u32[]{:S(2)}, u32[]{:S(2)}) collective-permute-start(f32[3,128]{1,0:T(4,128)S(1)} %bitcast.207), channel_id=1, source_target_pairs={{0,8},{8,0},{1,9},{9,1},{2,10},{10,2},{3,11},{11,3},{4,12},{12,4},... | collective-permute-start | bytes 4616 | tf_op jit(solution)/shard_map/ppermute | solution.py:22
  317.4 14.6 %collective-permute-start.4 = (f32[3,128]{1,0:T(4,128)S(1)}, f32[3,128]{1,0:T(4,128)S(1)}, u32[]{:S(2)}, u32[]{:S(2)}) collective-permute-start(f32[3,128]{1,0:T(4,128)S(1)} %bitcast.208), channel_id=1, source_target_pairs={{0,16},{16,0},{1,17},{17,1},{2,18},{18,2},{3,19},{19,3},{4,20},{20... | collective-permute-start | bytes 4616 | tf_op jit(solution)/shard_map/ppermute | solution.py:22
  471.5 174.8 %copy-start.14 = (s32[1024]{0:T(1024)S(1)}, s32[1024]{0:T(1024)}, u32[]{:S(2)}) copy-start(s32[1024]{0:T(1024)} %copy-done.13) | copy-start | bytes 12292
  471.5 178.1 %copy-start.10 = (s32[2048,1]{0,1:T(1,128)S(1)}, s32[2048,1]{0,1:T(1,128)}, u32[]{:S(2)}) copy-start(s32[2048,1]{0,1:T(1,128)} %param.31) | copy-start | bytes 24580
  471.5 186.0 %copy-start.6 = (s32[640]{0:T(1024)S(1)}, s32[640]{0:T(1024)}, u32[]{:S(2)}) copy-start(s32[640]{0:T(1024)} %copy-done.4) | copy-start | bytes 7684
  649.5 2.5 collective-permute-start.5
  650.3 3.6 collective-permute-start.6
  650.9 3.6 collective-permute-start.7
  651.5 3.6 collective-permute-start.8
  652.0 4.5 collective-permute-start.9
  794.9 176.6 %copy-start.19 = (s32[2048]{0:T(1024)S(1)}, s32[2048]{0:T(1024)}, u32[]{:S(2)}) copy-start(s32[2048]{0:T(1024)} %param.30) | copy-start | bytes 24580
  971.4 11.0 collective-permute-start.10
  977.2 5.2 collective-permute-start.11
  978.7 3.7 collective-permute-start.12
  980.4 3.6 collective-permute-start.13
  982.0 4.5 collective-permute-start.14
  1027.2 18.2 %all-to-all-start = ((f32[10,32,256]{2,0,1:T(8,128)}), f32[10,32,256]{2,0,1:T(8,128)S(1)}, u32[]{:S(2)}, u32[]{:S(2)}) async-start(f32[10,32,256]{2,0,1:T(8,128)} %copy.329), calls=%async_computation | async-start | bytes 1048576 | tf_op jit(solution)/shard_map/all_to_all | solution.py:125
  1109.7 61.7 %all-to-all-start.1 = ((f32[3,32,256]{2,0,1:T(4,128)}), f32[3,32,256]{2,0,1:T(4,128)S(1)}, u32[]{:S(2)}, u32[]{:S(2)}) async-start(f32[3,32,256]{2,0,1:T(4,128)} %get-tuple-element.29), calls=%async_computation.1 | async-start | bytes 262144 | tf_op jit(solution)/shard_map/all_to_all | solution.py:138
  (18 other events, 376.0 us)
where the time goes:
time: 1270 us; the launch traced here: 1260 us
  other arithmetic  667 us (53%)
  local copies, waits for them, and re-layouts  507 us (40%)
  blocking collectives  40.1 us (3%)
  waiting for transfers between devices  24.1 us (2%)
  starting transfers between devices  21 us (2%)
    scatter-add x3, other arithmetic, element_forces(): return jnp.zeros_like(nodal_field).at[:, corners.reshape(-1)].add(forces....  524 us
    gather x6, local copies, waits for them, and re-layouts, element_forces(): gathered = nodal_field[:, corners].reshape(24, blocks, 128)  356 us
    scatter-add x1, other arithmetic, per_device(): contact_force.at[:, master_index.reshape(-1)].add(-pushed.reshape(3, -1))  56.1 us
    psum x1, blocking collectives, per_device(): lax.psum(jax.ops.segment_sum(jnp.concatenate([weighted, net_force, cross_...  40.1 us
    gather x2, local copies, waits for them, and re-layouts, per_device(): positions[:, master_index]  32.3 us
    gather x2, local copies, waits for them, and re-layouts, per_device(): speeds[:, master_index]  30.8 us
    reshape x6, local copies, waits for them, and re-layouts, element_forces(): forces.reshape(3, 8 * corners.shape[1])  26.3 us
  transfers between devices with their start and end apart: 17, of which 7 were waited for; matrix products, arithmetic and copies ran while one was open for 6% of the time, Pallas kernels for 0%

commit v1 on v0

--- a/solution.py
+++ b/solution.py
@@ -145,13 +145,16 @@
     net_force = ext_force - assembled + contact_force - node_mass[None] * accel_column
     part_index = jnp.minimum(part_of_node, PARTS_SIZE)
     weighted = jnp.concatenate([node_mass[None], node_mass[None] * positions], 0)
-    totals = lax.psum(
-        jax.ops.segment_sum(
-            jnp.concatenate([weighted, net_force, cross_product(positions, net_force)], 0).T,
-            part_index,
-            PARTS_SIZE + 1,
-        )[:PARTS_SIZE].T,
-        "dom",
+    totals = jnp.sum(
+        lax.all_gather(
+            jax.ops.segment_sum(
+                jnp.concatenate([weighted, net_force, cross_product(positions, net_force)], 0).T,
+                part_index,
+                PARTS_SIZE + 1,
+            )[:PARTS_SIZE].T,
+            "dom",
+        ),
+        axis=0,
     )
     mass_total = part_mass + totals[0]
     centre = (part_mass[None] * part_center + totals[1:4]) / mass_total[None]

time: 1270 us -> 1280 us (level)
    all_gather x0 -> x1, blocking collectives: none -> 44.8 us  [per_device(): lax.all_gather(jax.ops.segment_sum(jnp.concatenate([weighted, net_force,...]
    psum x1 -> x0, blocking collectives: 40.1 us -> none  [per_device(): lax.psum(jax.ops.segment_sum(jnp.concatenate([weighted, net_force, cross_...]
where the time goes in v1:
time: 1280 us; the launch traced here: 1270 us
  other arithmetic  667 us (52%)
  local copies, waits for them, and re-layouts  505 us (39%)
  blocking collectives  44.8 us (4%)
  waiting for transfers between devices  24.1 us (2%)
  starting transfers between devices  21 us (2%)
    scatter-add x3, other arithmetic, element_forces(): return jnp.zeros_like(nodal_field).at[:, corners.reshape(-1)].add(forces....  524 us
    gather x6, local copies, waits for them, and re-layouts, element_forces(): gathered = nodal_field[:, corners].reshape(24, blocks, 128)  355 us
    scatter-add x1, other arithmetic, per_device(): contact_force.at[:, master_index.reshape(-1)].add(-pushed.reshape(3, -1))  56.1 us
    all_gather x1, blocking collectives, per_device(): lax.all_gather(jax.ops.segment_sum(jnp.concatenate([weighted, net_force,...  44.8 us
    gather x2, local copies, waits for them, and re-layouts, per_device(): positions[:, master_index]  32.2 us
    gather x2, local copies, waits for them, and re-layouts, per_device(): speeds[:, master_index]  30.6 us
    reshape x6, local copies, waits for them, and re-layouts, element_forces(): forces.reshape(3, 8 * corners.shape[1])  26.3 us
  transfers between devices with their start and end apart: 17, of which 7 were waited for; matrix products, arithmetic and copies ran while one was open for 6% of the time, Pallas kernels for 0%

profile of v1, /device:TPU:0, one launch (start us, length us, event | category | flops | bytes accessed | tf_op | source)
XLA Modules:
  0.0 1267.0 jit_solution(6049074356317821737)
XLA Ops:
  5.1 108.5 %gather_fusion = f32[32768,3]{1,0:T(8,128)} fusion(f32[3,4096]{0,1:T(8,128)S(1)} %copy.353, s32[32768]{0:T(1024)S(1)} %broadcast_clamp_fusion), kind=kCustom, calls=%fused_computation | custom fusion | bytes 917504 | tf_op jit(solution)/shard_map/gather | solution.py:34
  113.6 9.8 copy.354
  124.7 8.6 copy.359
  133.4 174.7 %scatter_custom_fusion = f32[3,4096]{0,1:T(8,128)S(1)} fusion(s32[32768]{0:T(1024)S(1)} %bitcast.189, f32[32768,3]{1,0:T(8,128)} %copy.359, f32[]{:T(128)} %constant.76.clone.1), kind=kCustom, calls=%fused_computation.32 | custom fusion | flops 98304 | bytes 49664 | tf_op jit(solution)/shard_map/scatter-add | solution.py:39
  319.5 9.1 reduce-window.6
  332.5 7.7 scatter_fusion
  342.3 108.5 %gather_fusion.2 = f32[32768,3]{1,0:T(8,128)} fusion(f32[3,4096]{0,1:T(8,128)S(1)} %copy.367, s32[32768]{0:T(1024)S(1)} %broadcast_clamp_fusion), kind=kCustom, calls=%fused_computation.2 | custom fusion | bytes 917504 | tf_op jit(solution)/shard_map/gather | solution.py:34
  450.8 9.8 copy.368
  461.9 8.6 copy.372
  470.5 174.7 %scatter_custom_fusion.2 = f32[3,4096]{0,1:T(8,128)S(1)} fusion(s32[32768]{0:T(1024)S(1)} %bitcast.190, f32[32768,3]{1,0:T(8,128)} %copy.372, f32[]{:T(128)} %constant.76.clone.1), kind=kCustom, calls=%fused_computation.30 | custom fusion | flops 98304 | bytes 49664 | tf_op jit(solution)/shard_map/scatter-add | solution.py:39
  656.4 7.4 scatter_fusion.1
  665.2 108.5 %gather_fusion.4 = f32[32768,3]{1,0:T(8,128)} fusion(f32[3,4096]{0,1:T(8,128)S(1)} %copy.380, s32[32768]{0:T(1024)S(1)} %broadcast_clamp_fusion), kind=kCustom, calls=%fused_computation.4 | custom fusion | bytes 917504 | tf_op jit(solution)/shard_map/gather | solution.py:34
  773.7 9.8 copy.381
  784.8 8.6 copy.385
  793.4 174.7 %scatter_custom_fusion.4 = f32[3,4096]{0,1:T(8,128)S(1)} fusion(s32[32768]{0:T(1024)S(1)} %bitcast.191, f32[32768,3]{1,0:T(8,128)} %copy.385, f32[]{:T(128)} %constant.76.clone.1), kind=kCustom, calls=%fused_computation.28 | custom fusion | flops 98304 | bytes 49664 | tf_op jit(solution)/shard_map/scatter-add | solution.py:39
  1003.1 7.0 gather_fusion.6
  1012.3 9.8 scatter_fusion.3
  1028.4 15.6 %all-to-all-done = f32[10,32,256]{2,0,1:T(8,128)S(1)} async-done(((f32[10,32,256]{2,0,1:T(8,128)}), f32[10,32,256]{2,0,1:T(8,128)S(1)}, u32[]{:S(2)}, u32[]{:S(2)}) %all-to-all-start) | async-done | bytes 327712 | tf_op jit(solution)/shard_map/all_to_all | solution.py:125
  1044.1 29.3 %gather_fusion.8 = f32[8192,3]{1,0:T(8,128)} fusion(f32[3,4096]{0,1:T(8,128)} %copy.395, s32[8192]{0:T(1024)S(1)} %broadcast_clamp_fusion.1), kind=kCustom, calls=%fused_computation.8 | custom fusion | bytes 229376 | tf_op jit(solution)/shard_map/gather | solution.py:132
  1073.4 27.7 %gather_fusion.9 = f32[8192,3]{1,0:T(8,128)} fusion(f32[3,4096]{0,1:T(8,128)S(1)} %copy.396, s32[8192]{0:T(1024)S(1)} %broadcast_clamp_fusion.1), kind=kCustom, calls=%fused_computation.9 | custom fusion | bytes 229376 | tf_op jit(solution)/shard_map/gather | solution.py:133
  1113.4 56.1 %scatter_custom_fusion.7 = f32[3,4096]{0,1:T(8,128)S(1)} fusion(s32[8192]{0:T(1024)S(1)} %bitcast.202, f32[8192,3]{1,0:T(8,128)} %copy.406, f32[]{:T(128)} %constant.76.clone.1), kind=kCustom, calls=%fused_computation.26 | custom fusion | flops 24576 | bytes 49664 | tf_op jit(solution)/shard_map/scatter-add | solution.py:141
  1172.2 24.1 %scatter_custom_fusion.8 = f32[3,4096]{0,1:T(8,128)S(1)} fusion(f32[3,4096]{0,1:T(8,128)S(1)} %scatter_custom_fusion.7, s32[2048]{0:T(1024)} %get-tuple-element.63, f32[3,8192]{0,1:T(8,128)} %bitcast.168, s32[2048]{0:T(1024)S(1)} %broadcast_clamp_fusion.2), kind=kCustom, calls=%fused_computation.24 | custom fusion | flops 6144 | bytes 49152 | tf_op jit(solution)/shard_map/scatter-add | solution.py:143
  1198.5 22.4 %scatter_custom_fusion.9 = f32[401,10]{1,0:T(8,128)S(1)} fusion(s32[4096]{0:T(1024)S(1)} %broadcast_minimum_fusion, f32[4096,10]{1,0:T(8,128)S(1)} %copy.410, f32[]{:T(128)} %constant.76.clone.1), kind=kCustom, calls=%fused_computation.61 | custom fusion | flops 40960 | bytes 16044 | tf_op jit(solution)/shard_map/scatter-add | solution.py:150
  1221.0 44.8 %all-gather.1 = f32[32,10,400]{2,1,0:T(8,128)S(1)} all-gather(f32[1,10,400]{2,1,0:T(8,128)S(1)} %copy.411), channel_id=2, replica_groups=mesh['dom'=32] {'dom'}, dimensions={0}, use_global_device_ids=true | all-gather | bytes 528000 | tf_op jit(solution)/shard_map/all_gather | solution.py:149
  (206 shorter events, 99.4 us)
Async XLA Ops:
  133.3 186.2 %copy-start.9 = (s32[2048,1]{0,1:T(1,128)S(1)}, s32[2048,1]{0,1:T(1,128)}, u32[]{:S(2)}) copy-start(s32[2048,1]{0,1:T(1,128)} %param.31) | copy-start | bytes 24580
  133.3 176.5 %copy-start.4 = (s32[640]{0:T(1024)}, s32[640]{0:T(1024)S(1)}, u32[]{:S(2)}) copy-start(s32[640]{0:T(1024)S(1)} %fusion.33) | copy-start | bytes 7684
  133.4 186.2 %copy-start.13 = (s32[1024]{0:T(1024)}, s32[1024]{0:T(1024)S(1)}, u32[]{:S(2)}) copy-start(s32[1024]{0:T(1024)S(1)} %pad_clamp_fusion) | copy-start | bytes 12292
  310.5 19.7 %collective-permute-start = (f32[3,128]{1,0:T(4,128)}, f32[3,128]{1,0:T(4,128)}, u32[]{:S(2)}, u32[]{:S(2)}) collective-permute-start(f32[3,128]{1,0:T(4,128)} %bitcast.10), channel_id=1, source_target_pairs={{0,1},{1,0},{2,3},{3,2},{4,5},{5,4},{6,7},{7,6},{8,9},{9,8},{10,11... | collective-permute-start | bytes 4616 | tf_op jit(solution)/shard_map/ppermute | solution.py:22
  311.1 19.8 %collective-permute-start.1 = (f32[3,128]{1,0:T(4,128)S(1)}, f32[3,128]{1,0:T(4,128)}, u32[]{:S(2)}, u32[]{:S(2)}) collective-permute-start(f32[3,128]{1,0:T(4,128)S(1)} %bitcast.210), channel_id=1, source_target_pairs={{0,2},{2,0},{1,3},{3,1},{4,6},{6,4},{5,7},{7,5},{8,10},{10,8},{9,1... | collective-permute-start | bytes 4616 | tf_op jit(solution)/shard_map/ppermute | solution.py:22
  313.6 17.9 %collective-permute-start.2 = (f32[3,128]{1,0:T(4,128)S(1)}, f32[3,128]{1,0:T(4,128)S(1)}, u32[]{:S(2)}, u32[]{:S(2)}) collective-permute-start(f32[3,128]{1,0:T(4,128)S(1)} %bitcast.209), channel_id=1, source_target_pairs={{0,4},{4,0},{1,5},{5,1},{2,6},{6,2},{3,7},{7,3},{8,12},{12,8},{9,1... | collective-permute-start | bytes 4616 | tf_op jit(solution)/shard_map/ppermute | solution.py:22
  315.2 16.3 %collective-permute-start.3 = (f32[3,128]{1,0:T(4,128)S(1)}, f32[3,128]{1,0:T(4,128)S(1)}, u32[]{:S(2)}, u32[]{:S(2)}) collective-permute-start(f32[3,128]{1,0:T(4,128)S(1)} %bitcast.207), channel_id=1, source_target_pairs={{0,8},{8,0},{1,9},{9,1},{2,10},{10,2},{3,11},{11,3},{4,12},{12,4},... | collective-permute-start | bytes 4616 | tf_op jit(solution)/shard_map/ppermute | solution.py:22
  316.9 14.7 %collective-permute-start.4 = (f32[3,128]{1,0:T(4,128)S(1)}, f32[3,128]{1,0:T(4,128)S(1)}, u32[]{:S(2)}, u32[]{:S(2)}) collective-permute-start(f32[3,128]{1,0:T(4,128)S(1)} %bitcast.208), channel_id=1, source_target_pairs={{0,16},{16,0},{1,17},{17,1},{2,18},{18,2},{3,19},{19,3},{4,20},{20... | collective-permute-start | bytes 4616 | tf_op jit(solution)/shard_map/ppermute | solution.py:22
  470.4 174.8 %copy-start.14 = (s32[1024]{0:T(1024)S(1)}, s32[1024]{0:T(1024)}, u32[]{:S(2)}) copy-start(s32[1024]{0:T(1024)} %copy-done.13) | copy-start | bytes 12292
  470.5 178.1 %copy-start.10 = (s32[2048,1]{0,1:T(1,128)S(1)}, s32[2048,1]{0,1:T(1,128)}, u32[]{:S(2)}) copy-start(s32[2048,1]{0,1:T(1,128)} %param.31) | copy-start | bytes 24580
  470.5 186.0 %copy-start.6 = (s32[640]{0:T(1024)S(1)}, s32[640]{0:T(1024)}, u32[]{:S(2)}) copy-start(s32[640]{0:T(1024)} %copy-done.4) | copy-start | bytes 7684
  648.5 2.5 collective-permute-start.5
  649.3 3.6 collective-permute-start.6
  649.9 3.6 collective-permute-start.7
  650.5 3.6 collective-permute-start.8
  651.0 4.5 collective-permute-start.9
  793.4 176.6 %copy-start.19 = (s32[2048]{0:T(1024)S(1)}, s32[2048]{0:T(1024)}, u32[]{:S(2)}) copy-start(s32[2048]{0:T(1024)} %param.30) | copy-start | bytes 24580
  969.9 10.9 collective-permute-start.10
  975.6 5.2 collective-permute-start.11
  977.2 3.7 collective-permute-start.12
  978.8 3.6 collective-permute-start.13
  980.5 4.5 collective-permute-start.14
  1025.7 18.2 %all-to-all-start = ((f32[10,32,256]{2,0,1:T(8,128)}), f32[10,32,256]{2,0,1:T(8,128)S(1)}, u32[]{:S(2)}, u32[]{:S(2)}) async-start(f32[10,32,256]{2,0,1:T(8,128)} %copy.400), calls=%async_computation | async-start | bytes 1048576 | tf_op jit(solution)/shard_map/all_to_all | solution.py:125
  1107.9 61.7 %all-to-all-start.1 = ((f32[3,32,256]{2,0,1:T(4,128)}), f32[3,32,256]{2,0,1:T(4,128)S(1)}, u32[]{:S(2)}, u32[]{:S(2)}) async-start(f32[3,32,256]{2,0,1:T(4,128)} %get-tuple-element.31), calls=%async_computation.1 | async-start | bytes 262144 | tf_op jit(solution)/shard_map/all_to_all | solution.py:138
  (18 other events, 385.7 us)
